TPU v7x, 256 devices: a whole 4x4x8 slice. The times are simulated.
256 devices in a mesh: gr: 16 (over z, core), gc: 16 (over x, y).
Axes of the slice: x: 4, y: 4, z: 8, core: 2. Of those that a mesh axis runs over, the one named last changes fastest.
Arguments:
- out_grad: bfloat16 [131072, 512], P(('gr', 'gc')), may hold values from -6 to 6
- preactivation_state: bfloat16 [131072, 512], P(('gr', 'gc')), may hold values from -6 to 6
- features: bfloat16 [131072, 512], P(('gc', 'gr')), may hold values from -24 to 24
- weight: bfloat16 [512, 512], replicated, may hold values from -0.25 to 0.25
- block_values: bfloat16 [16, 16, 152, 128, 128], P('gr', 'gc'), may hold values from -0.1875 to 0.1875
- block_rows: int32 [16, 16, 152], P('gr', 'gc'), may hold values from 0 to 63, as said below
- block_cols: int32 [16, 16, 152], P('gr', 'gc'), may hold values from 0 to 63, as said below
- block_counts: int32 [16, 16], P('gr', 'gc'), may hold values from 1 to 152, as said below
Outputs:
- input_grad: bfloat16 [131072, 512], P(('gc', 'gr'))
- weight_grad: float32 [512, 512], replicated
Inputs may be any that keep to these rules, and one draw needn't show every extreme that they name: `block_rows`: block row within a tile; some entry equals 63. `block_cols`: block column within a tile; some entry equals 63. `block_counts`: slots from this count on are unused; some tile uses all 152 slots.
All inputs are finite; a program needn't handle non-finite values.
Results may differ from a plain program's by a relative error of at most 0.014.
Values may be sent and summed in bfloat16 or wider, within the bound.
A program may use at most 128 MiB of HBM per device.

v0:
```python
import math

import jax
import jax.numpy as jnp
from jax import lax
from jax.sharding import PartitionSpec as P


def local(
    out_grad,
    preactivation_state,
    features,
    weight,
    block_values,
    block_rows,
    block_cols,
    block_counts,
):
    masked = jnp.where(preactivation_state > 0, out_grad, jnp.zeros_like(out_grad))
    tile_grads = lax.all_gather(masked, "gc", axis=0, tiled=True)
    block_size = block_values.shape[-1]
    feature_width = masked.shape[1]
    stacked = tile_grads.reshape(-1, block_size, feature_width)
    values_here = block_values[0, 0]
    rows_here = block_rows[0, 0]
    cols_here = block_cols[0, 0]
    count_here = block_counts[0, 0]
    capacity = values_here.shape[0]
    group_size = math.gcd(capacity, 16)
    node_rows = features.shape[0]
    col_count = node_rows * lax.axis_size("gr") // block_size

    def summing_group(current_index, value_partial_sum):
        offset = current_index * group_size
        current_values = lax.dynamic_slice_in_dim(values_here, offset, group_size, 0)
        rows_now = lax.dynamic_slice_in_dim(rows_here, offset, group_size, 0)
        cols_now = lax.dynamic_slice_in_dim(cols_here, offset, group_size, 0)
        selected_entries = stacked[rows_now]
        contribution = jnp.einsum(
            "yql,yqa->yla", current_values, selected_entries, preferred_element_type=jnp.float32
        )
        active = offset + jnp.arange(group_size) < count_here
        contribution = jnp.where(active[:, None, None], contribution, jnp.zeros_like(contribution))
        return value_partial_sum.at[cols_now].add(contribution)

    value_partial_sum = lax.fori_loop(
        0,
        capacity // group_size,
        summing_group,
        jnp.zeros((col_count, block_size, feature_width), jnp.float32),
    )
    value_partial_sum = value_partial_sum.reshape(-1, feature_width)
    column_total = lax.psum(value_partial_sum.astype(jnp.bfloat16), "gr").astype(jnp.float32)
    mine = lax.dynamic_slice_in_dim(column_total, lax.axis_index("gr") * node_rows, node_rows, 0)
    spread = mine.astype(jnp.bfloat16)
    input_grad = lax.dot_general(
        spread, weight, (((1,), (1,)), ((), ())), preferred_element_type=jnp.float32
    ).astype(jnp.bfloat16)
    weight_term = lax.dot_general(
        features, spread, (((0,), (0,)), ((), ())), preferred_element_type=jnp.float32
    )
    scale_factor = (node_rows * lax.axis_size("gr") * lax.axis_size("gc")) ** (-0.5)
    weight_grad = lax.psum(weight_term, ("gr", "gc")) * scale_factor
    return (input_grad, weight_grad)


def solution(mesh):
    in_specs = (
        P(("gr", "gc"), None),
        P(("gr", "gc"), None),
        P(("gc", "gr"), None),
        P(),
        P("gr", "gc", None, None, None),
        P("gr", "gc", None),
        P("gr", "gc", None),
        P("gr", "gc"),
    )
    out_specs = (P(("gc", "gr"), None), P())
    return jax.shard_map(local, mesh=mesh, in_specs=in_specs, out_specs=out_specs, check_vma=False)
```

profile of v0, /device:TPU:2, one launch (start us, length us, event | category | flops | bytes accessed | tf_op | source)
XLA Modules:
  0.0 739.5 jit_solution(15906717005274415228)
XLA Ops:
  7.2 2.1 compare_select_fusion.2
  9.4 7.7 %copy.10 = bf16[1,1,152,128,128]{3,4,2,1,0:T(8,128)(2,1)} copy(bf16[1,1,152,128,128]{4,3,2,1,0:T(8,128)(2,1)} %param.14) | data formatting | bytes 9961472 | tf_op args[4]
  17.1 72.7 %all-gather.2.cloned.1.call-done = bf16[8192,512]{1,0:T(8,128)(2,1)} async-done(((bf16[512,512]{1,0:T(8,128)(2,1)}), bf16[8192,512]{1,0:T(8,128)(2,1)}) %all-gather.2.cloned.1.call-update) | async-done | bytes 8388624 | tf_op jit(solution)/shard_map/all_gather | solution.py:20
  89.8 7.9 %broadcast_in_dim.38 = f32[64,128,512]{2,1,0:T(8,128)} broadcast(f32[]{:T(128)} %constant.51.clone.1), dimensions={} | broadcast | bytes 16777220 | tf_op jit(solution)/shard_map/broadcast_in_dim | solution.py:50
  97.7 224.6 %while.13 = (s32[]{:T(128)}, f32[64,128,512]{2,1,0:T(8,128)}, s32[152]{0:T(256)S(1)}, s32[]{:T(128)}, bf16[152,128,128]{1,2,0:T(8,128)(2,1)}, /*index=5*/s32[152...) while((s32[]{:T(128)}, f32[64,128,512]{2,1,0:T(8,128)}, ...), condition=%wide.region_2.3_spmd, body=%wide.region_0.2_spmd.sunk | while | flops 135267392 | bytes 11800995 | solution.py:46
  97.8 5.0 gather_fusion
  105.1 4.5 scatter_fusion
  109.7 5.0 gather_fusion
  117.0 4.4 scatter_fusion
  121.5 5.0 gather_fusion
  128.8 4.4 scatter_fusion
  133.4 5.0 gather_fusion
  140.7 4.3 scatter_fusion
  145.1 5.0 gather_fusion
  152.5 4.4 scatter_fusion
  156.9 5.0 gather_fusion
  164.3 4.4 scatter_fusion
  168.8 5.0 gather_fusion
  176.2 4.3 scatter_fusion
  180.6 5.0 gather_fusion
  187.9 4.4 scatter_fusion
  192.4 5.0 gather_fusion
  199.8 4.4 scatter_fusion
  204.3 5.0 gather_fusion
  211.6 4.3 scatter_fusion
  216.0 5.0 gather_fusion
  223.4 4.4 scatter_fusion
  227.8 5.0 gather_fusion
  235.2 4.4 scatter_fusion
  239.6 5.0 gather_fusion
  247.0 4.5 scatter_fusion
  251.5 5.0 gather_fusion
  258.9 4.4 scatter_fusion
  263.3 5.0 gather_fusion
  270.7 4.3 scatter_fusion
  275.1 5.0 gather_fusion
  282.4 4.4 scatter_fusion
  286.9 5.0 gather_fusion
  294.3 4.4 scatter_fusion
  298.8 5.0 gather_fusion
  306.2 4.4 scatter_fusion
  310.7 5.0 gather_fusion
  318.0 4.3 scatter_fusion
  322.3 9.0 %convert_element_type.15 = bf16[64,128,512]{2,1,0:T(8,128)(2,1)} convert(f32[64,128,512]{2,1,0:T(8,128)} %get-tuple-element.126) | non-fusion elementwise | flops 4194304 | bytes 25165824 | tf_op jit(solution)/shard_map/convert_element_type | solution.py:53
  331.4 134.5 %all-reduce.3.cloned.1.call-done = bf16[8192,512]{1,0:T(8,128)(2,1)} async-done(((bf16[8192,512]{1,0:T(8,128)(2,1)}), bf16[8192,512]{1,0:T(8,128)(2,1)}) %all-reduce.3.cloned.1.call-update) | async-done | bytes 8388624 | tf_op jit(solution)/shard_map/psum | solution.py:53
  466.0 2.5 convolution_bitcast_fusion
  468.5 2.3 convolution_convert_fusion
  470.8 259.5 %all-reduce.5.cloned.1.call-done = f32[512,512]{0,1:T(8,128)} async-done(((f32[512,512]{0,1:T(8,128)}), f32[512,512]{0,1:T(8,128)}) %all-reduce.5.cloned.1.call-update) | async-done | bytes 1048592 | tf_op jit(solution)/shard_map/psum | solution.py:63
  (92 shorter events, 49.7 us)
Async XLA Ops:
  7.2 458.8 %copy-start = (bf16[512,512]{1,0:T(8,128)(2,1)S(1)}, bf16[512,512]{1,0:T(8,128)(2,1)}, u32[]{:S(2)}) copy-start(bf16[512,512]{1,0:T(8,128)(2,1)} %param.12) | copy-start | bytes 1572868
  7.2 82.6 %all-gather.2.cloned.1.call-start = ((), (), s32[]{:S(2)}) async-start(), calls=%async_computation | async-start | bytes 8912896 | tf_op jit(solution)/shard_map/all_gather | solution.py:20
  9.3 456.6 %all-reduce.3.cloned.1.call-start = ((), (), s32[]{:S(2)}) async-start(), calls=%async_computation.1 | async-start | bytes 16777216 | tf_op jit(solution)/shard_map/psum | solution.py:53
  89.8 7.9 %copy-start.2 = (s32[1,1,152]{2,1,0:T(1,128)S(1)}, s32[1,1,152]{2,1,0:T(1,128)}, u32[]{:S(2)}) copy-start(s32[1,1,152]{2,1,0:T(1,128)} %param.16) | copy-start | bytes 1828
  89.8 7.9 %copy-start.3 = (s32[1,1,152]{2,1,0:T(1,128)S(1)}, s32[1,1,152]{2,1,0:T(1,128)}, u32[]{:S(2)}) copy-start(s32[1,1,152]{2,1,0:T(1,128)} %param.15) | copy-start | bytes 1828
  331.3 137.1 %copy-start.1 = (bf16[512,512]{1,0:T(8,128)(2,1)S(1)}, bf16[512,512]{1,0:T(8,128)(2,1)}, u32[]{:S(2)}) copy-start(bf16[512,512]{1,0:T(8,128)(2,1)} %param.13) | copy-start | bytes 1572868
  331.4 398.9 %all-reduce.5.cloned.1.call-start = ((), (), s32[]{:S(2)}) async-start(), calls=%async_computation.2 | async-start | bytes 2097152 | tf_op jit(solution)/shard_map/psum | solution.py:63
Sparse Core Ops, SparseCore 0:
  11.0 78.7 all-gather.1
  331.5 134.4 all-reduce.2
  472.0 258.2 all-reduce.4
where the time goes:
time: 742 us; the launch traced here: 739 us
  waiting for transfers between devices  467 us (63%)
  local copies, waits for them, and re-layouts  111 us (15%)
  other arithmetic  110 us (15%)
  matrix products  37.8 us (5%)
  between operations  13.8 us (2%)
    psum x1, waiting for transfers between devices, local(): weight_grad = lax.psum(weight_term, ('gr', 'gc')) * scale_factor  260 us
    psum x1, waiting for transfers between devices, local(): lax.psum(value_partial_sum.astype(jnp.bfloat16), 'gr').astype(jnp.float32)  135 us
    gather x19, local copies, waits for them, and re-layouts, summing_group(): selected_entries = stacked[rows_now]  94.3 us
    scatter-add x19, other arithmetic, summing_group(): return value_partial_sum.at[cols_now].add(contribution)  83.2 us
    all_gather x1, waiting for transfers between devices, local(): tile_grads = lax.all_gather(masked, 'gc', axis=0, tiled=True)  72.7 us
    dot_general x19, matrix products, summing_group(): jnp.einsum('yql,yqa->yla', current_values, selected_entries, preferred_el...  33 us
  transfers between devices with their start and end apart: 3, of which 3 were waited for; matrix products, arithmetic and copies ran while one was open for 1% of the time, Pallas kernels for 0%

commit v1 on v0

v1 whole, which is shorter than its diff:
```python
import functools

import jax
import jax.numpy as jnp
from jax import lax
from jax.experimental import pallas as pl
from jax.experimental.pallas import tpu as pltpu
from jax.sharding import PartitionSpec as P

MESH = pl.DeviceIdType.MESH
F32, BF16 = jnp.float32, jnp.bfloat16
NX, NY, NZ = 4, 4, 8
NXY = NX * NY
BLOCK = 128
BPD = 4
CHUNKS = 4
UNROLL = 4
GROUPS = ((0, 1, 2), (3,))


def gather_messages():
    table = {}

    def add(key, axis, sign, owner, first, count):
        table[key] = (len(table), axis, sign, owner, first, count)

    for h in (0, 1):
        first = 2 * h

        def at(u, v):
            return (u, v) if h == 0 else (v, u)

        u_axis, v_axis = (0, 1) if h == 0 else (1, 0)
        add((h, "m1", 1), u_axis, 1, at(0, 0), first, 2)
        add((h, "m1", -1), u_axis, -1, at(0, 0), first, 2)
        add((h, "m2", 1), u_axis, 1, at(-1, 0), first, 1)
        add((h, "m2", -1), u_axis, -1, at(1, 0), first + 1, 1)
        for j in (0, -1, 1, 2):
            add((h, "n1", 1, j), v_axis, 1, at(j, 0), first, 2)
            add((h, "n1", -1, j), v_axis, -1, at(j, 0), first, 2)
            add((h, "n2", 1, j), v_axis, 1, at(j, -1), first, 1)
            add((h, "n2", -1, j), v_axis, -1, at(j, 1), first + 1, 1)
    return table


GATHER = gather_messages()


def kernel(slots, aux, og, state, feat, w, vals, ig, wg,
           xt, a, r, pp, sib, cs, cr, st, ft, bufs, sems):
    gr, gc = lax.axis_index("gr"), lax.axis_index("gc")
    z, core = lax.div(gr, 2), lax.rem(gr, 2)
    x, y = lax.div(gc, NY), lax.rem(gc, NY)
    dc = xt[0].shape[1]
    gsend, grecv, psend, precv, csend, crecv, vsem, wsems = sems
    pending = []

    def mesh_at(dx=0, dy=0, dz=0, other=False):
        c = 1 - core if other else core
        return {
            "gr": lax.rem(z + dz + NZ, NZ) * 2 + c,
            "gc": lax.rem(x + dx + NX, NX) * NY + lax.rem(y + dy + NY, NY),
        }

    def xy_peer(i):
        return {"gr": gr, "gc": lax.rem(gc + i, NXY)}

    def remote(src, dst, send, recv, device):
        return pltpu.make_async_remote_copy(
            src_ref=src, dst_ref=dst, send_sem=send, recv_sem=recv,
            device_id=device, device_id_type=MESH)

    def start(copy):
        copy.start()
        pending.append(copy)

    def gmsg(k, key):
        index, axis, sign, (ox, oy), first, count = GATHER[key]
        owner = lax.rem(x + ox + NX, NX) * NY + lax.rem(y + oy + NY, NY)
        ref = xt[k].at[pl.ds(owner * BPD + first, count)]
        device = mesh_at(dx=sign) if axis == 0 else mesh_at(dy=sign)
        return remote(ref, ref, gsend.at[k, index], grecv.at[k, index], device)

    def mask(k):
        for b in range(BPD):
            rows, cols = slice(b * BLOCK, (b + 1) * BLOCK), slice(k * dc, (k + 1) * dc)
            kept = jnp.where(state[rows, cols] > 0, og[rows, cols], jnp.zeros((BLOCK, dc), BF16))
            xt[k][gc * BPD + b] = kept.T

    def e0(k):
        for h in (0, 1):
            for sign in (1, -1):
                start(gmsg(k, (h, "m1", sign)))
        for h in (0, 1):
            for sign in (1, -1):
                start(gmsg(k, (h, "n1", sign, 0)))

    def e1(k):
        for h in (0, 1):
            for sign in (1, -1):
                gmsg(k, (h, "m1", sign)).wait_recv()
                start(gmsg(k, (h, "m2", sign)))
                start(gmsg(k, (h, "n1", 1, -sign)))
                start(gmsg(k, (h, "n1", -1, -sign)))
        for h in (0, 1):
            for sign in (1, -1):
                gmsg(k, (h, "n1", sign, 0)).wait_recv()
                start(gmsg(k, (h, "n2", sign, 0)))

    def e2(k):
        for h in (0, 1):
            gmsg(k, (h, "m2", 1)).wait_recv()
            gmsg(k, (h, "m2", -1)).wait_recv()
            start(gmsg(k, (h, "n1", 1, 2)))
            start(gmsg(k, (h, "n1", -1, 2)))
        for j in (-1, 1):
            for h in (0, 1):
                for sign in (1, -1):
                    gmsg(k, (h, "n1", sign, j)).wait_recv()
                    start(gmsg(k, (h, "n2", sign, j)))

    def e3(k):
        for h in (0, 1):
            for sign in (1, -1):
                gmsg(k, (h, "n1", sign, 2)).wait_recv()
                start(gmsg(k, (h, "n2", sign, 2)))

    def e4(k):
        for j in (0, -1, 1, 2):
            for h in (0, 1):
                for sign in (1, -1):
                    gmsg(k, (h, "n2", sign, j)).wait_recv()

    def product(k, low, high):
        def step(i, carry):
            s = i * UNROLL
            terms = [jnp.dot(xt[k][aux[s + t]], a[s + t], preferred_element_type=F32) for t in range(UNROLL)]
            for t in range(UNROLL):
                r[s + 1 + t] = r[aux[slots + s + t]] + terms[t]
            return carry

        lax.fori_loop(low, high, step, 0)

    def collect(k, c):
        def step(i, carry):
            for b in range(BPD):
                pp[k, c, i, b] = r[aux[2 * slots + (i * 2 + c) * BPD + b]].astype(BF16)
            return carry

        lax.fori_loop(0, NZ, step, 0)

    def pair_copy(k):
        return remote(pp.at[k, 1 - core], sib.at[k], psend.at[k], precv.at[k], mesh_at(other=True))

    def chain_copy(k, d, s):
        part = pl.ds(2 * d, 2) if s == 0 else pl.ds(0, BPD)
        return remote(cs.at[k, d, s, part], cr.at[k, d, s, part], csend.at[k, d, s], crecv.at[k, d, s],
                      mesh_at(dz=1 if d == 0 else -1))

    def chain(k, s):
        if s == 0:
            pair_copy(k).wait_recv()
        for d in (0, 1):
            far = NZ // 2 - s
            target = lax.rem(z + (far if d == 0 else NZ - far), NZ)
            if s > 0:
                chain_copy(k, d, s - 1).wait_recv()
            half = (2 * d, 2 * d + 1)
            for b in half if s == 0 else range(BPD):
                total = pp[k, core, target, b].astype(F32) + sib[k, target, b].astype(F32)
                if s > 1 or (s == 1 and b in half):
                    total = total + cr[k, d, s - 1, b].astype(F32)
                cs[k, d, s, b] = total.astype(BF16)
            start(chain_copy(k, d, s))

    def settle(k):
        for d in (0, 1):
            chain_copy(k, d, 3).wait_recv()
        for b in range(BPD):
            total = pp[k, core, z, b].astype(F32) + sib[k, z, b].astype(F32)
            total = total + cr[k, 0, 3, b].astype(F32) + cr[k, 1, 3, b].astype(F32)
            st[k * dc:(k + 1) * dc, b * BLOCK:(b + 1) * BLOCK] = total.astype(BF16)
        term = lax.dot_general(ft[...], st[k * dc:(k + 1) * dc, :], (((1,), (1,)), ((), ())),
                               preferred_element_type=F32)
        for n, group in enumerate(GROUPS):
            if k in group:
                bufs[n][0][:, :, group.index(k)] = term.astype(BF16).reshape(2, NXY, 16, dc)

    def wmsg(n, kind, i=0):
        own, fromsib, mine, got, zgot, out = bufs[n]
        s_send, s_recv = wsems[n]
        if kind == "pair":
            return remote(own.at[1 - core], fromsib, s_send.at[0], s_recv.at[0], mesh_at(other=True))
        if kind == "xy":
            return remote(mine.at[lax.rem(gc + i, NXY)], got.at[gc], s_send.at[i], s_recv.at[i], xy_peer(i))
        if kind == "z":
            return remote(zgot.at[z], zgot.at[z], s_send.at[NXY + i], s_recv.at[NXY + i], mesh_at(dz=i))
        if kind == "back":
            return remote(out.at[core, gc], out.at[core, gc], s_send.at[NXY + NZ + i], s_recv.at[NXY + NZ + i],
                          xy_peer(i))
        return remote(out.at[core], out.at[core], s_send.at[NXY + NZ], s_recv.at[NXY + NZ], mesh_at(other=True))

    def w0(n):
        start(wmsg(n, "pair"))

    def w1(n):
        own, fromsib, mine, got, zgot, out = bufs[n]
        wmsg(n, "pair").wait_recv()
        mine[...] = (own[core].astype(F32) + fromsib[...].astype(F32)).astype(BF16)
        for i in range(1, NXY):
            start(wmsg(n, "xy", i))
        got[gc] = mine[gc]

    def w2(n):
        own, fromsib, mine, got, zgot, out = bufs[n]
        for i in range(1, NXY):
            wmsg(n, "xy", i).wait_recv()
        total = got[0].astype(F32)
        for q in range(1, NXY):
            total = total + got[q].astype(F32)
        zgot[z] = total.astype(zgot.dtype)
        for i in range(1, NZ):
            start(wmsg(n, "z", i))

    def w3(n):
        own, fromsib, mine, got, zgot, out = bufs[n]
        for i in range(1, NZ):
            wmsg(n, "z", i).wait_recv()
        total = zgot[0].astype(F32)
        for q in range(1, NZ):
            total = total + zgot[q].astype(F32)
        out[core, gc] = total.astype(out.dtype)
        for i in range(1, NXY):
            start(wmsg(n, "back", i))

    def w4(n):
        for i in range(1, NXY):
            wmsg(n, "back", i).wait_recv()
        start(wmsg(n, "last"))

    def w5(n):
        out = bufs[n][5]
        wmsg(n, "last").wait_recv()
        for g, k in enumerate(GROUPS[n]):
            wg[:, k * dc:(k + 1) * dc] = out[:, :, g].astype(F32).reshape(2 * NXY * 16, dc)

    load = pltpu.make_async_copy(vals, a, vsem)
    load.start()
    barrier = pltpu.get_barrier_semaphore()
    partners = [mesh_at(other=True)] + [mesh_at(dz=i) for i in range(1, NZ)] + [xy_peer(i) for i in range(1, NXY)]
    for device in partners:
        pl.semaphore_signal(barrier, inc=1, device_id=device, device_id_type=MESH)
    mask(0)
    pl.semaphore_wait(barrier, len(partners))
    e0(0)
    mask(1)
    e1(0)
    for k in range(2, CHUNKS):
        mask(k)
    e2(0)
    e0(1)
    ft[...] = feat[...].T
    r[0] = jnp.zeros(r.shape[1:], F32)
    e3(0)
    load.wait()
    e4(0)
    total_steps = slots // UNROLL
    pieces = 6
    cut = [total_steps * i // pieces for i in range(pieces + 1)]
    for k in range(CHUNKS):
        more = k + 1 < CHUNKS
        back = k > 0
        for i in range(pieces):
            product(k, cut[i], cut[i + 1])
            if i == 0:
                if back:
                    chain(k - 1, 1)
                if more:
                    e1(k + 1)
            if i == 1 and back:
                chain(k - 1, 2)
            if i == 2 and more:
                e2(k + 1)
                if k + 2 < CHUNKS:
                    e0(k + 2)
            if i == 3:
                if back:
                    chain(k - 1, 3)
                if more:
                    e3(k + 1)
            if i == 4 and back:
                settle(k - 1)
        collect(k, 1 - core)
        start(pair_copy(k))
        collect(k, core)
        if k == CHUNKS - 1:
            w0(0)
        chain(k, 0)
        if more:
            e4(k + 1)
    last = CHUNKS - 1
    chain(last, 1)
    w1(0)
    chain(last, 2)
    chain(last, 3)
    w2(0)
    settle(last)
    w0(1)
    w3(0)
    w1(1)
    ig[...] = lax.dot_general(st[...], w[...], (((0,), (1,)), ((), ())), preferred_element_type=F32).astype(BF16)
    w4(0)
    w2(1)
    w5(0)
    w3(1)
    w4(1)
    w5(1)
    for copy in pending:
        copy.wait_send()


def local(og, state, feat, w, vals, rows, cols, counts):
    slots = vals.shape[2]
    width = og.shape[1]
    dc = width // CHUNKS
    rows, cols, count = rows[0, 0], cols[0, 0], counts[0, 0]
    place = jnp.arange(slots, dtype=jnp.int32)
    columns = jnp.arange(BPD * NZ * 2, dtype=jnp.int32)
    wanted = jnp.concatenate([cols, columns])
    limit = jnp.concatenate([jnp.minimum(place, count), jnp.full_like(columns, count)])
    hit = (wanted[:, None] == cols[None, :]) & (place[None, :] < limit[:, None])
    latest = jnp.max(jnp.where(hit, place[None, :] + 1, 0), axis=1)
    aux = jnp.concatenate([rows, latest])

    def group_bufs(n):
        g = len(GROUPS[n])
        return (
            pltpu.VMEM((2, NXY, g, 16, dc), BF16),
            pltpu.VMEM((NXY, g, 16, dc), BF16),
            pltpu.VMEM((NXY, g, 16, dc), BF16),
            pltpu.VMEM((NXY, g, 16, dc), BF16),
            pltpu.VMEM((NZ, g, 16, dc), F32),
            pltpu.VMEM((2, NXY, g, 16, dc), BF16),
        )

    nm = len(GATHER)
    dma = pltpu.SemaphoreType.DMA
    ww = 2 * NXY + NZ
    vm = pl.BlockSpec(memory_space=pltpu.VMEM)
    ig, wg = pl.pallas_call(
        functools.partial(kernel, slots),
        out_shape=(jax.ShapeDtypeStruct((og.shape[0], w.shape[0]), BF16),
                   jax.ShapeDtypeStruct((feat.shape[1], width), F32)),
        in_specs=[pl.BlockSpec(memory_space=pltpu.SMEM), vm, vm, vm, vm, pl.BlockSpec(memory_space=pl.ANY)],
        out_specs=(vm, vm),
        scratch_shapes=[
            tuple(pltpu.VMEM((BPD * NXY, dc, BLOCK), BF16) for _ in range(CHUNKS)),
            pltpu.VMEM((slots, BLOCK, BLOCK), BF16),
            pltpu.VMEM((slots + 1, dc, BLOCK), F32),
            pltpu.VMEM((CHUNKS, 2, NZ, BPD, dc, BLOCK), BF16),
            pltpu.VMEM((CHUNKS, NZ, BPD, dc, BLOCK), BF16),
            pltpu.VMEM((CHUNKS, 2, 4, BPD, dc, BLOCK), BF16),
            pltpu.VMEM((CHUNKS, 2, 4, BPD, dc, BLOCK), BF16),
            pltpu.VMEM((width, og.shape[0]), BF16),
            pltpu.VMEM((feat.shape[1], feat.shape[0]), BF16),
            tuple(group_bufs(n) for n in range(len(GROUPS))),
            (dma((CHUNKS, nm)), dma((CHUNKS, nm)), dma((CHUNKS,)), dma((CHUNKS,)),
             dma((CHUNKS, 2, 4)), dma((CHUNKS, 2, 4)), dma,
             tuple((dma((ww,)), dma((ww,))) for _ in GROUPS)),
        ],
        compiler_params=pltpu.CompilerParams(
            collective_id=0, has_side_effects=True, vmem_limit_bytes=67043328),
    )(aux, og, state, feat, w, vals.reshape(vals.shape[2:]))
    nodes = og.shape[0] * lax.axis_size("gr") * lax.axis_size("gc")
    return ig, wg * (nodes ** -0.5)


def solution(mesh):
    in_specs = (
        P(("gr", "gc"), None),
        P(("gr", "gc"), None),
        P(("gc", "gr"), None),
        P(),
        P("gr", "gc", None, None, None),
        P("gr", "gc", None),
        P("gr", "gc", None),
        P("gr", "gc"),
    )
    out_specs = (P(("gc", "gr"), None), P())
    return jax.shard_map(local, mesh=mesh, in_specs=in_specs, out_specs=out_specs, check_vma=False)
```

time: 742 us -> 166 us (0.22)
  waiting for transfers between devices: 467 us -> 0 us
  Pallas kernels: 0 us -> 154 us
  local copies, waits for them, and re-layouts: 111 us -> 1.88 us
  other arithmetic: 110 us -> 5.2 us
  matrix products: 37.8 us -> 0 us
  between operations: 13.8 us -> 1.3 us
    psum x2 -> x0, waiting for transfers between devices: 394 us -> none  [the longest x1 260 us: local(): weight_grad = lax.psum(weight_term, ('gr', 'gc')) * scale_factor]
    pallas_call x0 -> x1, Pallas kernels: none -> 154 us  [local(): pl.pallas_call(functools.partial(kernel, slots), out_shape=(jax.ShapeDtyp...]
    gather x19 -> x0, local copies, waits for them, and re-layouts: 94.3 us -> none  [summing_group(): selected_entries = stacked[rows_now]]
    scatter-add x19 -> x0, other arithmetic: 83.2 us -> none  [summing_group(): return value_partial_sum.at[cols_now].add(contribution)]
    all_gather x1 -> x0, waiting for transfers between devices: 72.7 us -> none  [local(): tile_grads = lax.all_gather(masked, 'gc', axis=0, tiled=True)]
    dot_general x21 -> x0, matrix products: 37.8 us -> none  [the longest x19 33 us: summing_group(): jnp.einsum('yql,yqa->yla', current_values, selected_entries, preferred_el...]
    lt x19 -> x0, other arithmetic: 12.3 us -> none  [summing_group(): active = offset + jnp.arange(group_size) < count_here]
    convert_element_type x1 -> x0, other arithmetic: 9.03 us -> none  [local(): value_partial_sum.astype(jnp.bfloat16)]
  transfers between devices with their start and end apart: 3 -> 0, of which waited for: 3 -> 0; matrix products, arithmetic and copies ran while one was open for 1% -> 0% of each run, Pallas kernels for 0% -> 0%
where the time goes in v1:
time: 166 us; the launch traced here: 163 us
  Pallas kernels  154 us (93%)
  other arithmetic  5.2 us (3%)
  local copies, waits for them, and re-layouts  1.88 us (1%)
    pallas_call x1, Pallas kernels, local(): pl.pallas_call(functools.partial(kernel, slots), out_shape=(jax.ShapeDtyp...  154 us

profile of v1, /device:TPU:2, one launch (start us, length us, event | category | flops | bytes accessed | tf_op | source)
XLA Modules:
  0.0 162.5 jit_solution(15680213899347316687)
XLA Ops:
  1.3 0.8 pad_add_fusion.1
  2.1 0.8 select_reduce_fusion
  2.9 1.3 pad_add_fusion.aux
  4.2 154.2 %shard_map.95 = (bf16[512,512]{1,0:T(8,128)(2,1)}, f32[512,512]{1,0:T(8,128)}) custom-call(s32[368]{0:T(512)} %pad_add_fusion.aux, bf16[512,512]{1,0:T(8,128)(2,1)} %og.1, bf16[512,512]{1,0:T(8,128)(2,1)} %state.1, bf16[512,512]{1,0:T(8,128)(2,1)} %feat.1, bf16[512,512]{1,0:T(8,128)(2,1)} %w.1, bf16[152,128,128]{2,1,0:T(8,128)(2,1)} %bitcast.6), custom_call_target="tpu_custom_call" | custom-call | tf_op jit(solution)/shard_map/pallas_call | solution.py:350
  158.4 2.3 %broadcast_multiply_fusion = f32[512,512]{1,0:T(8,128)} fusion(f32[512,512]{1,0:T(8,128)} %get-tuple-element.5), kind=kLoop, calls=%fused_computation | loop fusion | flops 262144 | bytes 2097152 | tf_op jit(solution)/shard_map/mul | solution.py:375
  160.7 1.9 %copy.12 = bf16[512,512]{1,0:T(8,128)(2,1)} copy(bf16[512,512]{1,0:T(8,128)(2,1)} %get-tuple-element.8) | data formatting | bytes 1048576
  (4 shorter events, 0.0 us)
